TPU v7x, 256 devices: a whole 4x4x8 slice. The times are simulated.
256 devices in a mesh: seq: 64 (over x_hi, y, z), head: 4 (over x_lo, core).
Axes of the slice: x: 4 (x_hi: 2, x_lo: 2; x = x_hi * 2 + x_lo), y: 4, z: 8, core: 2. Of those that a mesh axis runs over, the one named last changes fastest.
Arguments:
- queries: bfloat16 [98304, 2048], P('seq', 'head'), may hold values from -200 to 200
- keys_values: bfloat16 [2, 98304, 2048], P(None, 'seq', 'head'), may hold values from -6 to 6
- global_ids: int32 [2], replicated, may hold values from 0 to 1535
- rand_ids: int32 [1536, 3], replicated, may hold values from 0 to 1535, as said below
- out_weight: bfloat16 [2048, 4096], P(None, 'head'), may hold values from -2 to 2
Outputs:
- projected: bfloat16 [98304, 4096], P('seq', 'head')
Inputs may be any that keep to these rules, and one draw needn't show every extreme that they name: `rand_ids`: row i lists the 3 random key blocks of query block i. Among the 24 rows of one seq shard, at most 2 listed blocks lie on any one shard, and at most 1 of one column do; both bounds are reached.
All inputs are finite; a program needn't handle non-finite values.
Results may differ from a plain program's by a relative error of at most 0.0057.
Values may be sent and summed in bfloat16 or wider, within the bound.
A program may use at most 128 MiB of HBM per device.

v0:
```python
import jax
import jax.numpy as jnp
from jax import lax
from jax.sharding import PartitionSpec as P

HEAD_DIM = 128
BLOCK = 64
NGLOBAL = 2
NRANDOM = 3
group_blocks = 8


def padded_2(block, sides, width):
    for axis, dim in sides:
        count = lax.axis_size(axis)
        forward = [(i, i + 1) for i in range(count - 1)]
        backward = [(target, source) for source, target in forward]
        low = lax.ppermute(
            lax.slice_in_dim(block, block.shape[dim] - width, None, axis=dim), axis, forward
        )
        high = lax.ppermute(lax.slice_in_dim(block, 0, width, axis=dim), axis, backward)
        block = jnp.concatenate([low, block, high], axis=dim)
    return block


def broadcast(block, axis, owner):
    block = jnp.where(lax.axis_index(axis) == owner, block, jnp.zeros_like(block))
    return lax.psum(block, axis)


def plan_slots(requests, myself, capacity, per_shard):
    sources = requests // per_shard
    offsets = requests % per_shard
    count = requests.shape[1]
    order = jnp.arange(count, dtype=jnp.int32)
    earlier = (order[:, None] < order[None, :]).astype(jnp.int32)
    matches = (sources[:, :, None] == sources[:, None, :]).astype(jnp.int32)
    ranks = jnp.sum(matches * earlier[None], axis=1)
    slot_range = jnp.arange(capacity, dtype=jnp.int32)
    wanted = (
        (sources == myself)[:, None, :] & (ranks[:, None, :] == slot_range[None, :, None])
    ).astype(jnp.int32)
    chosen = jnp.sum(wanted * offsets[:, None, :], axis=2).reshape(-1)
    own_sources = lax.dynamic_index_in_dim(sources, myself, 0, keepdims=False)
    own_ranks = lax.dynamic_index_in_dim(ranks, myself, 0, keepdims=False)
    return (chosen, own_sources * capacity + own_ranks)


def attend_blocks(query_part, local_keys, local_values, glob_keys, glob_values, valid):
    scale = 1.0 / HEAD_DIM**0.5
    near_scores = (
        jnp.einsum("bqhd,bkhd->bhqk", query_part, local_keys, preferred_element_type=jnp.float32)
        * scale
    )
    near_scores = jnp.where(valid[:, None, None, :], near_scores, -jnp.inf)
    glob_scores = (
        jnp.einsum("bqhd,khd->bhqk", query_part, glob_keys, preferred_element_type=jnp.float32)
        * scale
    )
    highest = jnp.maximum(jnp.max(near_scores, axis=-1), jnp.max(glob_scores, axis=-1))
    near_exp = jnp.exp(near_scores - highest[..., None])
    glob_exp = jnp.exp(glob_scores - highest[..., None])
    total = jnp.sum(near_exp, axis=-1) + jnp.sum(glob_exp, axis=-1)
    near_weights = (near_exp / total[..., None]).astype(jnp.bfloat16)
    glob_weights = (glob_exp / total[..., None]).astype(jnp.bfloat16)
    mixed = jnp.einsum(
        "bhqk,bkhd->bqhd", near_weights, local_values, preferred_element_type=jnp.float32
    )
    mixed = mixed + jnp.einsum(
        "bhqk,khd->bqhd", glob_weights, glob_values, preferred_element_type=jnp.float32
    )
    return mixed.astype(jnp.bfloat16)


def body(queries, keys_values, global_ids, rand_ids, out_weight):
    rows = queries.shape[0]
    width = queries.shape[1]
    heads_here = width // HEAD_DIM
    local_blocks = rows // BLOCK
    shards = lax.axis_size("seq")
    myself = lax.axis_index("seq")
    total_blocks = local_blocks * shards
    pair_blocks = keys_values.reshape(2, local_blocks, BLOCK, width)
    padded = padded_2(keys_values, (("seq", 1),), BLOCK)
    padded = padded.reshape(2, local_blocks + 2, BLOCK, width)
    panel_list = []
    for which in range(NGLOBAL):
        target = global_ids[which]
        owner = target // local_blocks
        local_panel = lax.dynamic_index_in_dim(
            pair_blocks, target % local_blocks, 1, keepdims=False
        )
        panel_list.append(broadcast(local_panel, "seq", owner))
    glob = jnp.stack(panel_list, axis=1).reshape(2, NGLOBAL * BLOCK, heads_here, HEAD_DIM)
    requests = rand_ids.reshape(shards, local_blocks, NRANDOM)
    capacity = (local_blocks + shards - 1) // shards
    fetched = []
    for column in range(NRANDOM):
        chosen, slots = plan_slots(requests[:, :, column], myself, capacity, local_blocks)
        outgoing = jnp.take(pair_blocks, chosen, axis=1)
        incoming = lax.all_to_all(outgoing, "seq", split_axis=1, concat_axis=1, tiled=True)
        fetched.append(jnp.take(incoming, slots, axis=1))
    remote = jnp.stack(fetched, axis=2)
    segment = jnp.arange((3 + NRANDOM) * BLOCK, dtype=jnp.int32) // BLOCK

    def one_group(index):
        first = index * group_blocks
        query_part = lax.dynamic_slice_in_dim(queries, first * BLOCK, group_blocks * BLOCK, 0)
        query_part = query_part.reshape(group_blocks, BLOCK, heads_here, HEAD_DIM)
        window = lax.dynamic_slice_in_dim(padded, first, group_blocks + 2, 1)
        farther = lax.dynamic_slice_in_dim(remote, first, group_blocks, 1)
        farther = farther.reshape(2, group_blocks, NRANDOM * BLOCK, width)
        local = jnp.concatenate(
            [
                window[:, 0:group_blocks],
                window[:, 1 : group_blocks + 1],
                window[:, 2 : group_blocks + 2],
                farther,
            ],
            axis=2,
        )
        local = local.reshape(2, group_blocks, (3 + NRANDOM) * BLOCK, heads_here, HEAD_DIM)
        block_ids = myself * local_blocks + first + jnp.arange(group_blocks, dtype=jnp.int32)
        drop_before = (segment[None, :] == 0) & (block_ids[:, None] == 0)
        drop_after = (segment[None, :] == 2) & (block_ids[:, None] == total_blocks - 1)
        valid = jnp.logical_not(drop_before | drop_after)
        mixed = attend_blocks(query_part, local[0], local[1], glob[0], glob[1], valid)
        return mixed.reshape(group_blocks * BLOCK, width)

    attended = lax.map(
        one_group, jnp.arange(local_blocks // group_blocks, dtype=jnp.int32)
    ).reshape(rows, width)
    summed = jnp.dot(
        lax.all_gather(attended, "head", axis=1, tiled=True),
        out_weight,
        preferred_element_type=jnp.float32,
    )
    return summed.astype(jnp.bfloat16)


def solution(mesh):
    in_specs = (P("seq", "head"), P(None, "seq", "head"), P(), P(), P(None, "head"))
    out_specs = P("seq", "head")
    return jax.shard_map(body, mesh=mesh, in_specs=in_specs, out_specs=out_specs, check_vma=False)
```

profile of v0, /device:TPU:1, one launch (start us, length us, event | category | flops | bytes accessed | tf_op | source)
XLA Modules:
  0.0 1352.4 jit_solution(5042256346633394672)
XLA Ops:
  8.1 7.2 gather_fusion.2
  15.3 7.5 select_bitcast_fusion.1
  22.8 15.6 %all-to-all-start.1 = ((bf16[2,64,64,512]{3,2,0,1:T(8,128)(2,1)}), bf16[2,64,64,512]{3,2,0,1:T(8,128)(2,1)}, u32[]{:S(2)}, u32[]{:S(2)}) async-start(bf16[2,64,64,512]{3,2,0,1:T(8,128)(2,1)} %select_bitcast_fusion.1), calls=%async_computation.1 | async-start | bytes 16777216 | tf_op jit(solution)/shard_map/all_to_all | solution.py:101
  38.6 5.5 gather_fusion
  44.1 7.5 select_bitcast_fusion.2
  51.5 169.7 %all-to-all-done.1 = bf16[2,64,64,512]{3,2,0,1:T(8,128)(2,1)} async-done(((bf16[2,64,64,512]{3,2,0,1:T(8,128)(2,1)}), bf16[2,64,64,512]{3,2,0,1:T(8,128)(2,1)}, u32[]{:S(2)}, u32[]{:S(2)}) %all-to-all-start.1) | async-done | bytes 8388640 | tf_op jit(solution)/shard_map/all_to_all | solution.py:101
  221.2 12.9 all-to-all-start
  234.1 5.2 gather_fusion.4
  239.3 7.5 select_bitcast_fusion
  246.8 169.9 %all-to-all-done = bf16[2,64,64,512]{3,2,0,1:T(8,128)(2,1)} async-done(((bf16[2,64,64,512]{3,2,0,1:T(8,128)(2,1)}), bf16[2,64,64,512]{3,2,0,1:T(8,128)(2,1)}, u32[]{:S(2)}, u32[]{:S(2)}) %all-to-all-start) | async-done | bytes 8388640 | tf_op jit(solution)/shard_map/all_to_all | solution.py:101
  416.7 13.1 all-to-all-start.2
  429.9 2.8 collective-permute-start
  444.4 169.5 %collective-permute-done = bf16[2,64,512]{2,1,0:T(8,128)(2,1)S(1)} collective-permute-done((bf16[2,64,512]{2,1,0:T(8,128)(2,1)S(1)}, bf16[2,64,512]{2,1,0:T(8,128)(2,1)S(1)}, u32[]{:S(2)}, u32[]{:S(2)}) %collective-permute-start) | collective-permute-done | bytes 131104 | tf_op jit(solution)/shard_map/ppermute | solution.py:18
  615.6 2.7 pad_maximum_fusion.2
  618.3 454.0 %all-reduce.3.cloned.1.call-done = (bf16[2,1,64,512]{3,2,1,0:T(8,128)(2,1)}, bf16[2,1,64,512]{3,2,1,0:T(8,128)(2,1)}) async-done(((bf16[2,1,64,512]{3,2,1,0:T(8,128)(2,1)}, bf16[2,1,64,512]{3,2,1,0:T(8,128)(2,1)}), (bf16[2,1,64,512]{3,2,1,0:T(8,128)(2,1)}, bf16[2,1,64,512]{3,2,1,0:T(8,128)(2,1)})) %all-reduce.3.cloned.1.call-update) | async-done | bytes 262160 | tf_op jit(solution)/shard_map/psum | solution.py:28
  1073.4 7.7 copy.122
  1081.1 5.9 gather_fusion.3
  1087.0 7.7 copy.120
  1094.7 5.9 gather_fusion.1
  1100.6 2.4 select_bitcast_fusion.4
  1105.5 7.7 copy.124
  1113.2 5.9 gather_fusion.5
  1119.1 2.4 select_bitcast_fusion.3
  1121.9 4.2 pad_maximum_fusion.1
  1126.1 114.5 %while.14 = (s32[]{:T(128)}, bf16[3,512,512]{2,1,0:T(8,128)(2,1)}, s32[3]{0:T(128)S(1)}, bf16[2,26,64,512]{3,2,1,0:T(8,128)(2,1)}, bf16[2,24,3,64,512]{4,3,0,1,2...) while((s32[]{:T(128)}, bf16[3,512,512]{2,1,0:T(8,128)(2,1)}, ...), condition=%wide.region_13.16_spmd.clone.clone, body=%wide.region_8.15_spmd.clone.clone.sunk | while | flops 573845248 | bytes 120519192 | solution.py:130
  1127.2 2.3 constant_dynamic-slice_fusion.9
  1129.6 2.2 constant_dynamic-slice_fusion.8
  1132.2 4.8 pad_maximum_fusion.5
  1137.0 3.3 fusion.73
  1140.3 3.4 copy.164
  1153.8 4.8 copy.163
  1158.5 3.3 fusion.80
  1165.5 2.4 constant_dynamic-slice_fusion.9
  1167.8 2.2 constant_dynamic-slice_fusion.8
  1170.4 4.8 pad_maximum_fusion.5
  1175.2 3.3 fusion.73
  1178.6 3.4 copy.164
  1192.0 4.8 copy.163
  1196.8 3.3 fusion.80
  1203.7 2.1 constant_dynamic-slice_fusion.9
  1205.9 2.2 constant_dynamic-slice_fusion.8
  1208.5 4.8 pad_maximum_fusion.5
  1213.3 3.3 fusion.73
  1216.6 3.4 copy.164
  1230.0 4.8 copy.163
  1234.8 3.3 fusion.80
  1240.6 93.8 %all-gather.2.cloned.1.call-done = bf16[1536,2048]{1,0:T(8,128)(2,1)} async-done(((bf16[1536,512]{1,0:T(8,128)(2,1)}), bf16[1536,2048]{1,0:T(8,128)(2,1)}) %all-gather.2.cloned.1.call-update) | async-done | bytes 6291472 | tf_op jit(solution)/shard_map/all_gather | solution.py:134
  1334.4 11.1 convolution_convert_fusion
  (159 shorter events, 53.1 us)
Async XLA Ops:
  7.6 7.7 copy-start.8
  7.7 7.6 copy-start.9
  8.0 7.4 copy-start.11
  8.0 7.4 copy-start.12
  8.0 30.5 %copy-start.10 = (s32[64,24]{0,1:T(8,128)}, s32[64,24]{0,1:T(8,128)S(1)}, u32[]{:S(2)}) copy-start(s32[64,24]{0,1:T(8,128)S(1)} %get-tuple-element.222) | copy-start | bytes 18436
  22.8 15.7 %copy-start.2 = (bf16[2,1536,512]{2,1,0:T(8,128)(2,1)S(1)}, bf16[2,1536,512]{2,1,0:T(8,128)(2,1)}, u32[]{:S(2)}) copy-start(bf16[2,1536,512]{2,1,0:T(8,128)(2,1)} %param.12) | copy-start | bytes 9437188
  22.8 198.4 %all-to-all-start.1 = ((bf16[2,64,64,512]{3,2,0,1:T(8,128)(2,1)}), bf16[2,64,64,512]{3,2,0,1:T(8,128)(2,1)}, u32[]{:S(2)}, u32[]{:S(2)}) async-start(bf16[2,64,64,512]{3,2,0,1:T(8,128)(2,1)} %select_bitcast_fusion.1), calls=%async_computation.1 | async-start | bytes 16777216 | tf_op jit(solution)/shard_map/all_to_all | solution.py:101
  221.2 195.5 %all-to-all-start = ((bf16[2,64,64,512]{3,2,0,1:T(8,128)(2,1)}), bf16[2,64,64,512]{3,2,0,1:T(8,128)(2,1)}, u32[]{:S(2)}, u32[]{:S(2)}) async-start(bf16[2,64,64,512]{3,2,0,1:T(8,128)(2,1)} %select_bitcast_fusion.2), calls=%async_computation | async-start | bytes 16777216 | tf_op jit(solution)/shard_map/all_to_all | solution.py:101
  246.8 187.3 %copy-start.14 = (s32[2]{0:T(128)S(1)}, s32[2]{0:T(128)}, u32[]{:S(2)}) copy-start(s32[2]{0:T(128)} %param.13) | copy-start | bytes 28
  416.7 688.8 %all-to-all-start.2 = ((bf16[2,64,64,512]{3,2,0,1:T(8,128)(2,1)}), bf16[2,64,64,512]{3,2,0,1:T(8,128)(2,1)}, u32[]{:S(2)}, u32[]{:S(2)}) async-start(bf16[2,64,64,512]{3,2,0,1:T(8,128)(2,1)} %select_bitcast_fusion), calls=%async_computation.2 | async-start | bytes 16777216 | tf_op jit(solution)/shard_map/all_to_all | solution.py:101
  429.8 642.5 %all-reduce.3.cloned.1.call-start = ((), (), s32[]{:S(2)}) async-start(), calls=%async_computation.4 | async-start | bytes 524288 | tf_op jit(solution)/shard_map/psum | solution.py:28
  429.9 184.1 %collective-permute-start = (bf16[2,64,512]{2,1,0:T(8,128)(2,1)S(1)}, bf16[2,64,512]{2,1,0:T(8,128)(2,1)S(1)}, u32[]{:S(2)}, u32[]{:S(2)}) collective-permute-start(bf16[2,64,512]{2,1,0:T(8,128)(2,1)S(1)} %get-tuple-element.258), channel_id=1, source_target_pairs={{0,4},{4,8},{8,12},{12,16},{16,20},{20,24},{24,28},{28,32},{32,36}... | collective-permute-start | bytes 393224 | tf_op jit(solution)/shard_map/ppermute | solution.py:18
  432.7 182.9 %collective-permute-start.1 = (bf16[2,64,512]{2,1,0:T(8,128)(2,1)S(1)}, bf16[2,64,512]{2,1,0:T(8,128)(2,1)}, u32[]{:S(2)}, u32[]{:S(2)}) collective-permute-start(bf16[2,64,512]{2,1,0:T(8,128)(2,1)S(1)} %get-tuple-element.259), channel_id=1, source_target_pairs={{4,0},{8,4},{12,8},{16,12},{20,16},{24,20},{28,24},{32,28},{36,32}... | collective-permute-start | bytes 393224 | tf_op jit(solution)/shard_map/ppermute | solution.py:21
  439.1 895.4 %all-gather.2.cloned.1.call-start = ((), (), s32[]{:S(2)}) async-start(), calls=%async_computation.3 | async-start | bytes 7864320 | tf_op jit(solution)/shard_map/all_gather | solution.py:134
  1094.7 5.9 copy-start.13
  1100.6 2.8 copy-start.7
  1100.6 2.8 copy-start.15
  1119.1 2.8 copy-start.6
  1148.3 2.0 copy-start.3
  1150.2 1.6 copy-start
  1150.8 3.0 copy-start.4
  1153.7 4.8 copy-start.1
  1158.5 3.4 copy-start.5
  1186.5 2.0 copy-start.3
  1188.5 1.6 copy-start
  1189.0 3.0 copy-start.4
  1192.0 4.8 copy-start.1
  1196.8 3.4 copy-start.5
  1224.5 2.0 copy-start.3
  1226.5 1.6 copy-start
  1227.0 3.0 copy-start.4
  1230.0 4.8 copy-start.1
  1234.8 3.4 copy-start.5
Sparse Core Ops, SparseCore 0:
  439.2 633.0 all-reduce.2
  1240.8 93.6 all-gather.1
where the time goes:
time: 1350 us
  waiting for transfers between devices  1060 us (79%)
  local copies, waits for them, and re-layouts  131 us (10%)
  other arithmetic  63.6 us (5%)
  starting transfers between devices  46.1 us (3%)
  matrix products  31.4 us (2%)
  between operations  17.4 us (1%)
    psum x1, waiting for transfers between devices, broadcast(): return lax.psum(block, axis)  454 us
    all_to_all x3, waiting for transfers between devices, body(): lax.all_to_all(outgoing, 'seq', split_axis=1, concat_axis=1, tiled=True)  340 us
    ppermute x1, waiting for transfers between devices, padded_2(): lax.ppermute(lax.slice_in_dim(block, block.shape[dim] - width, None, axis...  170 us
    all_gather x1, waiting for transfers between devices, body(): lax.all_gather(attended, 'head', axis=1, tiled=True)  93.8 us
    all_to_all x3, starting transfers between devices, body(): lax.all_to_all(outgoing, 'seq', split_axis=1, concat_axis=1, tiled=True)  41.7 us
  transfers between devices with their start and end apart: 7, of which 6 were waited for; matrix products, arithmetic and copies ran while one was open for 5% of the time, Pallas kernels for 0%

commit v1 on v0

--- a/solution.py
+++ b/solution.py
@@ -25,7 +25,7 @@
 
 def broadcast(block, axis, owner):
     block = jnp.where(lax.axis_index(axis) == owner, block, jnp.zeros_like(block))
-    return lax.psum(block, axis)
+    return jnp.sum(lax.all_gather(block, axis), axis=0)
 
 
 def plan_slots(requests, myself, capacity, per_shard):

time: 1350 us -> 948 us (0.70)
  waiting for transfers between devices: 1060 us -> 632 us
    psum x1 -> x0, waiting for transfers between devices: 454 us -> none  [broadcast(): return lax.psum(block, axis)]
    all_to_all x3, waiting for transfers between devices: 340 us -> 388 us  [body(): lax.all_to_all(outgoing, 'seq', split_axis=1, concat_axis=1, tiled=True)]
    all_gather x1, waiting for transfers between devices: 93.8 us -> 74.9 us  [body(): lax.all_gather(attended, 'head', axis=1, tiled=True)]
  transfers between devices with their start and end apart: 7 -> 8, of which waited for: 6 -> 5; matrix products, arithmetic and copies ran while one was open for 5% -> 8% of each run, Pallas kernels for 0% -> 0%
where the time goes in v1:
time: 948 us; the launch traced here: 946 us
  waiting for transfers between devices  632 us (67%)
  local copies, waits for them, and re-layouts  132 us (14%)
  other arithmetic  71.7 us (8%)
  starting transfers between devices  57.4 us (6%)
  matrix products  31.4 us (3%)
  between operations  17.5 us (2%)
    all_to_all x3, waiting for transfers between devices, body(): lax.all_to_all(outgoing, 'seq', split_axis=1, concat_axis=1, tiled=True)  388 us
    ppermute x1, waiting for transfers between devices, padded_2(): lax.ppermute(lax.slice_in_dim(block, block.shape[dim] - width, None, axis...  162 us
    all_gather x1, waiting for transfers between devices, body(): lax.all_gather(attended, 'head', axis=1, tiled=True)  74.9 us
    all_to_all x3, starting transfers between devices, body(): lax.all_to_all(outgoing, 'seq', split_axis=1, concat_axis=1, tiled=True)  53 us
    all_to_all x3, local copies, waits for them, and re-layouts, body(): lax.all_to_all(outgoing, 'seq', split_axis=1, concat_axis=1, tiled=True)  23.3 us
    select_n x5, other arithmetic, body(): outgoing = jnp.take(pair_blocks, chosen, axis=1)  22.5 us
    slice x6, local copies, waits for them, and re-layouts, one_group(): local[0]  20.2 us
  transfers between devices with their start and end apart: 8, of which 5 were waited for; matrix products, arithmetic and copies ran while one was open for 8% of the time, Pallas kernels for 0%

profile of v1, /device:TPU:1, one launch (start us, length us, event | category | flops | bytes accessed | tf_op | source)
XLA Modules:
  0.0 946.4 jit_solution(8225001316482457517)
XLA Ops:
  8.1 7.2 gather_fusion.2
  15.3 7.5 select_bitcast_fusion.1
  22.8 15.6 %all-to-all-start.1 = ((bf16[2,64,64,512]{3,2,0,1:T(8,128)(2,1)}), bf16[2,64,64,512]{3,2,0,1:T(8,128)(2,1)}, u32[]{:S(2)}, u32[]{:S(2)}) async-start(bf16[2,64,64,512]{3,2,0,1:T(8,128)(2,1)} %select_bitcast_fusion.1), calls=%async_computation.1 | async-start | bytes 16777216 | tf_op jit(solution)/shard_map/all_to_all | solution.py:101
  44.1 5.6 gather_fusion
  49.7 7.6 select_bitcast_fusion.2
  57.2 191.7 %all-to-all-done.1 = bf16[2,64,64,512]{3,2,0,1:T(8,128)(2,1)} async-done(((bf16[2,64,64,512]{3,2,0,1:T(8,128)(2,1)}), bf16[2,64,64,512]{3,2,0,1:T(8,128)(2,1)}, u32[]{:S(2)}, u32[]{:S(2)}) %all-to-all-start.1) | async-done | bytes 8388640 | tf_op jit(solution)/shard_map/all_to_all | solution.py:101
  249.0 19.2 %all-to-all-start = ((bf16[2,64,64,512]{3,2,0,1:T(8,128)(2,1)}), bf16[2,64,64,512]{3,2,0,1:T(8,128)(2,1)}, u32[]{:S(2)}, u32[]{:S(2)}) async-start(bf16[2,64,64,512]{3,2,0,1:T(8,128)(2,1)} %select_bitcast_fusion.2), calls=%async_computation | async-start | bytes 16777216 | tf_op jit(solution)/shard_map/all_to_all | solution.py:101
  269.0 5.2 gather_fusion.4
  274.2 7.5 select_bitcast_fusion
  281.7 196.4 %all-to-all-done = bf16[2,64,64,512]{3,2,0,1:T(8,128)(2,1)} async-done(((bf16[2,64,64,512]{3,2,0,1:T(8,128)(2,1)}), bf16[2,64,64,512]{3,2,0,1:T(8,128)(2,1)}, u32[]{:S(2)}, u32[]{:S(2)}) %all-to-all-start) | async-done | bytes 8388640 | tf_op jit(solution)/shard_map/all_to_all | solution.py:101
  478.1 18.1 %all-to-all-start.2 = ((bf16[2,64,64,512]{3,2,0,1:T(8,128)(2,1)}), bf16[2,64,64,512]{3,2,0,1:T(8,128)(2,1)}, u32[]{:S(2)}, u32[]{:S(2)}) async-start(bf16[2,64,64,512]{3,2,0,1:T(8,128)(2,1)} %select_bitcast_fusion), calls=%async_computation.2 | async-start | bytes 16777216 | tf_op jit(solution)/shard_map/all_to_all | solution.py:101
  496.2 2.8 collective-permute-start
  505.6 162.2 %collective-permute-done = bf16[2,64,512]{2,1,0:T(8,128)(2,1)S(1)} collective-permute-done((bf16[2,64,512]{2,1,0:T(8,128)(2,1)S(1)}, bf16[2,64,512]{2,1,0:T(8,128)(2,1)S(1)}, u32[]{:S(2)}, u32[]{:S(2)}) %collective-permute-start) | collective-permute-done | bytes 131104 | tf_op jit(solution)/shard_map/ppermute | solution.py:18
  667.8 6.1 collective-permute-done.1
  673.9 2.7 pad_maximum_fusion.2
  676.6 4.6 bitcast_reduce_fusion.1
  681.2 4.6 bitcast_reduce_fusion
  686.0 7.8 copy.122
  693.7 5.9 gather_fusion.3
  699.6 7.8 copy.120
  707.4 5.8 gather_fusion.1
  713.3 2.4 select_bitcast_fusion.4
  718.1 7.7 copy.124
  725.8 5.9 gather_fusion.5
  731.7 2.4 select_bitcast_fusion.3
  734.6 4.1 pad_maximum_fusion.1
  738.6 115.1 %while.14 = (s32[]{:T(128)}, bf16[3,512,512]{2,1,0:T(8,128)(2,1)}, s32[3]{0:T(128)S(1)}, bf16[2,26,64,512]{3,2,1,0:T(8,128)(2,1)}, bf16[2,24,3,64,512]{4,3,0,1,2...) while((s32[]{:T(128)}, bf16[3,512,512]{2,1,0:T(8,128)(2,1)}, ...), condition=%wide.region_13.16_spmd.clone.clone, body=%wide.region_8.15_spmd.clone.clone.sunk | while | flops 573845248 | bytes 120519192 | solution.py:130
  742.1 2.2 constant_dynamic-slice_fusion.8
  744.7 4.8 pad_maximum_fusion.5
  749.5 3.3 fusion.73
  752.8 3.4 copy.164
  766.3 4.8 copy.163
  771.1 3.3 fusion.80
  778.3 2.3 constant_dynamic-slice_fusion.9
  780.6 2.2 constant_dynamic-slice_fusion.8
  783.2 4.8 pad_maximum_fusion.5
  788.0 3.3 fusion.73
  791.3 3.4 copy.164
  804.8 4.8 copy.163
  809.6 3.3 fusion.80
  818.9 2.2 constant_dynamic-slice_fusion.8
  821.5 4.8 pad_maximum_fusion.5
  826.3 3.3 fusion.73
  829.6 3.4 copy.164
  843.2 4.8 copy.163
  848.0 3.3 fusion.80
  853.8 74.9 %all-gather.6.cloned.1.call-done = bf16[1536,2048]{1,0:T(8,128)(2,1)} async-done(((bf16[1536,512]{1,0:T(8,128)(2,1)}), bf16[1536,2048]{1,0:T(8,128)(2,1)}) %all-gather.6.cloned.1.call-update) | async-done | bytes 6291472 | tf_op jit(solution)/shard_map/all_gather | solution.py:134
  928.7 11.1 %convolution_convert_fusion = bf16[1536,1024]{1,0:T(8,128)(2,1)} fusion(bf16[1536,2048]{1,0:T(8,128)(2,1)} %all-gather.6.cloned.1.call-done, bf16[2048,1024]{1,0:T(8,128)(2,1)} %param.15), kind=kOutput, calls=%fused_computation.61 | convolution fusion | flops 6444023808 | bytes 13631488 | tf_op jit(solution)/shard_map/dot_general | solution.py:133
  (164 shorter events, 55.7 us)
Async XLA Ops:
  7.6 7.7 copy-start.8
  7.7 7.6 copy-start.9
  8.0 7.4 copy-start.11
  8.0 7.3 copy-start.12
  8.0 36.0 %copy-start.10 = (s32[64,24]{0,1:T(8,128)}, s32[64,24]{0,1:T(8,128)S(1)}, u32[]{:S(2)}) copy-start(s32[64,24]{0,1:T(8,128)S(1)} %get-tuple-element.222) | copy-start | bytes 18436
  22.8 15.7 %copy-start.14 = (s32[2]{0:T(128)S(1)}, s32[2]{0:T(128)}, u32[]{:S(2)}) copy-start(s32[2]{0:T(128)} %param.13) | copy-start | bytes 28
  22.8 20.4 %copy-start.2 = (bf16[2,1536,512]{2,1,0:T(8,128)(2,1)S(1)}, bf16[2,1536,512]{2,1,0:T(8,128)(2,1)}, u32[]{:S(2)}) copy-start(bf16[2,1536,512]{2,1,0:T(8,128)(2,1)} %param.12) | copy-start | bytes 9437188
  22.8 226.2 %all-to-all-start.1 = ((bf16[2,64,64,512]{3,2,0,1:T(8,128)(2,1)}), bf16[2,64,64,512]{3,2,0,1:T(8,128)(2,1)}, u32[]{:S(2)}, u32[]{:S(2)}) async-start(bf16[2,64,64,512]{3,2,0,1:T(8,128)(2,1)} %select_bitcast_fusion.1), calls=%async_computation.1 | async-start | bytes 16777216 | tf_op jit(solution)/shard_map/all_to_all | solution.py:101
  38.5 638.1 %all-gather.8.cloned.1.call-start = ((), (), s32[]{:S(2)}) async-start(), calls=%async_computation.4 | async-start | bytes 8519680 | tf_op jit(solution)/shard_map/all_gather | solution.py:28
  249.0 229.1 %all-to-all-start = ((bf16[2,64,64,512]{3,2,0,1:T(8,128)(2,1)}), bf16[2,64,64,512]{3,2,0,1:T(8,128)(2,1)}, u32[]{:S(2)}, u32[]{:S(2)}) async-start(bf16[2,64,64,512]{3,2,0,1:T(8,128)(2,1)} %select_bitcast_fusion.2), calls=%async_computation | async-start | bytes 16777216 | tf_op jit(solution)/shard_map/all_to_all | solution.py:101
  268.2 413.0 %all-gather.10.cloned.1.call-start = ((), (), s32[]{:S(2)}) async-start(), calls=%async_computation.5 | async-start | bytes 8519680 | tf_op jit(solution)/shard_map/all_gather | solution.py:28
  478.1 240.1 %all-to-all-start.2 = ((bf16[2,64,64,512]{3,2,0,1:T(8,128)(2,1)}), bf16[2,64,64,512]{3,2,0,1:T(8,128)(2,1)}, u32[]{:S(2)}, u32[]{:S(2)}) async-start(bf16[2,64,64,512]{3,2,0,1:T(8,128)(2,1)} %select_bitcast_fusion), calls=%async_computation.2 | async-start | bytes 16777216 | tf_op jit(solution)/shard_map/all_to_all | solution.py:101
  496.2 432.5 %all-gather.6.cloned.1.call-start = ((), (), s32[]{:S(2)}) async-start(), calls=%async_computation.3 | async-start | bytes 7864320 | tf_op jit(solution)/shard_map/all_gather | solution.py:134
  496.2 171.6 %collective-permute-start = (bf16[2,64,512]{2,1,0:T(8,128)(2,1)S(1)}, bf16[2,64,512]{2,1,0:T(8,128)(2,1)S(1)}, u32[]{:S(2)}, u32[]{:S(2)}) collective-permute-start(bf16[2,64,512]{2,1,0:T(8,128)(2,1)S(1)} %get-tuple-element.256), channel_id=1, source_target_pairs={{0,4},{4,8},{8,12},{12,16},{16,20},{20,24},{24,28},{28,32},{32,36}... | collective-permute-start | bytes 393224 | tf_op jit(solution)/shard_map/ppermute | solution.py:18
  499.1 174.8 %collective-permute-start.1 = (bf16[2,64,512]{2,1,0:T(8,128)(2,1)S(1)}, bf16[2,64,512]{2,1,0:T(8,128)(2,1)}, u32[]{:S(2)}, u32[]{:S(2)}) collective-permute-start(bf16[2,64,512]{2,1,0:T(8,128)(2,1)S(1)} %get-tuple-element.257), channel_id=1, source_target_pairs={{4,0},{8,4},{12,8},{16,12},{20,16},{24,20},{28,24},{32,28},{36,32}... | collective-permute-start | bytes 393224 | tf_op jit(solution)/shard_map/ppermute | solution.py:21
  707.4 5.8 copy-start.13
  713.3 2.8 copy-start.7
  713.3 2.8 copy-start.15
  731.7 2.8 copy-start.6
  760.9 2.0 copy-start.3
  762.8 1.6 copy-start
  763.4 3.0 copy-start.4
  766.3 4.8 copy-start.1
  771.1 3.4 copy-start.5
  799.3 2.0 copy-start.3
  801.3 1.6 copy-start
  801.8 3.0 copy-start.4
  804.8 4.8 copy-start.1
  809.6 3.4 copy-start.5
  837.7 2.0 copy-start.3
  839.6 1.6 copy-start
  840.2 3.0 copy-start.4
  843.2 4.8 copy-start.1
  847.9 3.4 copy-start.5
Sparse Core Ops, SparseCore 0:
  44.1 221.0 all-gather.7
  272.8 221.2 all-gather.9
  853.9 74.7 all-gather.5
